TPU v7x, 128 devices: a whole 4x4x4 slice. The times are simulated.
128 devices in a mesh: blk: 64 (over y, z, x_hi, core), grp: 2 (over x_lo).
Axes of the slice: x: 4 (x_hi: 2, x_lo: 2; x = x_hi * 2 + x_lo), y: 4, z: 4, core: 2. Of those that a mesh axis runs over, the one named last changes fastest.
Arguments:
- x_pos: float32 [8, 98304], P(None, ('blk', 'grp')), may hold values from -6 to 6, as said below
- y_pos: float32 [8, 98304], P(None, ('blk', 'grp')), may hold values from -6 to 6, as said below
- f_pot: float32 [98304], P(('blk', 'grp')), may hold values from -8 to 260
- g_pot: float32 [98304], P(('blk', 'grp')), may hold values from -8 to 260
- x_logw: float32 [98304], P(('blk', 'grp')), may hold values from -1.5 to 1.5
- y_logw: float32 [98304], P(('blk', 'grp')), may hold values from -1.5 to 1.5
Outputs:
- f_out: float32 [98304], P(('blk', 'grp'))
- g_out: float32 [98304], P(('blk', 'grp'))
Inputs may be any that keep to these rules, and one draw needn't show every extreme that they name: `x_pos`: states of both clouds. `y_pos`: states of both clouds.
All inputs are finite; a program needn't handle non-finite values.
Results may differ from a plain program's by a relative error of at most 0.0003.
Values sent between devices are 32-bit elements; how exact they have to be, the bound alone decides.
A program may use at most 64 MiB of HBM per device.

v0:
```python
import jax
import jax.numpy as jnp
from jax import lax
from jax.experimental import pallas as pl
from jax.experimental.pallas import tpu as pltpu
from jax.sharding import PartitionSpec as P

TILES = 6
ROWS = 56
SLOTS = 16
DEPTH = 64
LOG2E = 1.4426950408889634
LN2 = 0.6931471805599453
SMALL = 2.0**-80
LARGE = 2.0**120
lowest = -1e30
SLOT_PEERS = (
    (0, 0, 0), (0, 1, 0), (0, 0, 1), (0, 2, 1), (1, 0, 0), (1, 1, 0), (0, 1, 1), (0, 3, 1),
    (0, 2, 0), (0, 3, 0), (1, 0, 1), (1, 1, 1), (1, 2, 1), (1, 2, 0), (1, 3, 1), (1, 3, 0),
)
RELAY = {2: 6, 3: 7, 8: 9, 12: 14, 13: 15}
DIRECT = tuple(slot for slot in range(1, 16) if slot not in RELAY.values())
SHARED = 12
GROUPS = ((1,), (2, 3), (6, 7), (8, 9), (4, 5), (10, 11), (12,), (13,), (14,), (15,))
PASS_ON = {1: (2, 3), 2: (8,), 5: (12,), 6: (13,)}
NEAR_AFTER, NEAR_PASS_AFTER, FAR_AFTER = (2, 5, 1)
MESH = pl.DeviceIdType.MESH


def split3(a):
    high = a.astype(jnp.bfloat16).astype(jnp.float32)
    rest = a - high
    mid = rest.astype(jnp.bfloat16).astype(jnp.float32)
    return high, mid, rest - mid


def lines(values):
    shape = (8, values[0].shape[1])
    row = lax.broadcasted_iota(jnp.int32, shape, 0)
    out = jnp.zeros(shape, jnp.float32)
    for k, value in enumerate(values):
        out = jnp.where(row == k, value, out)
    return out


def other_terms(pos, bias):
    high, mid, low = split3(pos)
    one = jnp.ones_like(bias)
    last = lines([*split3(bias), one, one, one])
    return jnp.concatenate([high, high, high, mid, mid, low, last, jnp.zeros_like(pos)], axis=0)


def own_terms(pos, bias):
    high, mid, low = split3(pos * LOG2E)
    one = jnp.ones_like(bias)
    last = lines([one, one, one, *split3(bias)])
    return jnp.concatenate([high, mid, low, high, mid, high, last, jnp.zeros_like(pos)], axis=0)


def pack_shard(pos_ref, pot_ref, logw_ref, out_ref):
    for j in range(TILES):
        pos = pos_ref[:, 128 * j : 128 * j + 128]
        out_ref[8 * j : 8 * j + 8, :] = pos
        half = 0.5 * jnp.sum(pos * pos, axis=0, keepdims=True)
        bias = (logw_ref[j : j + 1, :] + pot_ref[j : j + 1, :] - half) * LOG2E
        out_ref[48 + j : 49 + j, :] = bias
    out_ref[54:56, :] = jnp.zeros((2, 128), jnp.float32)


def peer_table():
    block, line = lax.axis_index("blk"), lax.axis_index("grp")
    place = lax.rem(block, 4)
    core, high = lax.rem(place, 2), lax.div(place, 2)
    cores, highs = (core, 1 - core), (high, 1 - high)
    lines = (line, 1 - line)
    near, inward, outward = [], [], []
    for e in range(4):
        other = cores[e % 2] + 2 * highs[e // 2]
        base = block - place + other + 64
        near.append(block - place + other)
        inward.append(lax.rem(base + 4 - 8 * lax.div(other - place + 4, 4), 64))
        outward.append(lax.rem(base - 4 + 8 * lax.div(place - other + 4, 4), 64))

    def find(slot, out=False):
        zone, e, d = SLOT_PEERS[slot]
        return ((outward if out else inward)[e] if zone else near[e], lines[d])

    return find


def exchange_kernel(
    x_hbm, y_hbm, f_hbm, g_hbm, xl_hbm, yl_hbm,
    out_ref, yh_ref, xh_ref,
    xin, yin, fin, gin, xlin, ylin,
    xs, ys, ybuf, xbuf, xlhs, ylhs, rhs, racc, cacc, csend, cbuf,
    load, ysend, yrecv, xsend, xrecv, farsend, cs_sem, cr_sem, keep, ready,
):
    find = peer_table()
    barrier = pltpu.get_barrier_semaphore()
    greeted = [find(slot) for slot in (8, 3, 2, 4, 5, 1)] + [find(4, out=True)]
    for target in greeted:
        pl.semaphore_signal(barrier, inc=1, device_id=target, device_id_type=MESH)
    loads = [
        pltpu.make_async_copy(src, dst, load.at[k])
        for k, (src, dst) in enumerate(
            ((y_hbm, yin), (g_hbm, gin), (yl_hbm, ylin), (x_hbm, xin), (f_hbm, fin), (xl_hbm, xlin))
        )
    ]
    for copy in loads:
        copy.start()
    csend[...] = jnp.zeros_like(csend)
    racc[...] = jnp.zeros_like(racc)
    cacc[...] = jnp.zeros_like(cacc)
    for copy in loads:
        copy.wait()
    pack_shard(yin, gin, ylin, ys)
    pack_shard(xin, fin, xlin, xs)
    pl.semaphore_wait(barrier, len(greeted))

    def y_copy(slot, via=None):
        source = ys if via is None else ybuf.at[via]
        target = find(slot, out=True) if via is None else find(1)
        return pltpu.make_async_remote_copy(
            source, ybuf.at[slot], ysend, yrecv.at[slot], device_id=target, device_id_type=MESH
        )

    def x_copy(slot, via=None):
        target = find(slot) if via is None else find(1)
        if slot < SHARED:
            source = xs if via is None else xh_ref.at[via]
            return pltpu.make_async_remote_copy(
                source, xh_ref.at[slot], xsend, xrecv.at[slot], device_id=target, device_id_type=MESH
            )
        source = xs if via is None else xbuf.at[via - SHARED]
        return pltpu.make_async_remote_copy(
            source, xbuf.at[slot - SHARED], farsend, xrecv.at[slot], device_id=target, device_id_type=MESH
        )

    def c_copy(slot):
        return pltpu.make_async_remote_copy(
            csend.at[slot], cbuf.at[slot], cs_sem, cr_sem, device_id=find(slot), device_id_type=MESH
        )

    def all_of(ref, sem, start, size):
        part = ref.at[pl.ds(start, size)]
        return pltpu.make_async_copy(part, part, sem)

    def tell(slot, k):
        pl.semaphore_signal(ready.at[k], inc=1, device_id=find(slot), device_id_type=MESH)

    def send(slots):
        for slot in slots:
            y_copy(slot).start()
            if slot >= SHARED:
                x_copy(slot).start()

    for k, slot in ((2, 8), (0, 2), (1, 3)):
        tell(slot, k)
    send((4, 5, 2, 3, 1, 8))

    def own_side(shard, lhs):
        for j in range(TILES):
            terms = own_terms(shard[8 * j : 8 * j + 8, :], shard[48 + j : 49 + j, :])
            lhs[128 * j : 128 * j + 128, :] = terms.T.astype(jnp.bfloat16)

    own_side(xs, xlhs)

    def prepare(shard, spot):
        for j in range(TILES):
            terms = other_terms(shard[8 * j : 8 * j + 8, :], shard[48 + j : 49 + j, :])
            rhs[spot, :, 128 * j : 128 * j + 128] = terms.astype(jnp.bfloat16)

    def shared_tile(spot, slot):
        for c in range(3):
            weights = rhs[spot, :, 256 * c : 256 * c + 256]
            column = jnp.zeros((8, 256), jnp.float32)
            for t in range(0, 768, 128):
                score = jnp.dot(xlhs[t : t + 128, :], weights, preferred_element_type=jnp.float32)
                plan = jnp.exp2(score)
                column = column + jnp.sum(plan.reshape(16, 8, 256), axis=0)
                racc[t : t + 128, :] += plan[:, :128] + plan[:, 128:]
            total = jnp.sum(column, axis=0, keepdims=True)
            csend[slot, 2 * c : 2 * c + 1, :] = total[:, :128]
            csend[slot, 2 * c + 1 : 2 * c + 2, :] = total[:, 128:]

    def row_tile(spot, lhs, acc):
        for c in range(3):
            weights = rhs[spot, :, 256 * c : 256 * c + 256]
            for t in range(0, 768, 128):
                score = jnp.dot(lhs[t : t + 128, :], weights, preferred_element_type=jnp.float32)
                plan = jnp.exp2(score)
                acc[t : t + 128, :] += plan[:, :128] + plan[:, 128:]

    prepare(ys, 0)
    shared_tile(0, 0)
    pl.semaphore_wait(ready.at[0], 1)
    send((10, 11))
    pl.semaphore_wait(ready.at[1], 1)
    send((12,))
    pltpu.make_async_copy(xs, xh_ref.at[0], keep.at[0]).start()
    pltpu.make_async_copy(ys, yh_ref.at[0], keep.at[1]).start()
    own_side(ys, ylhs)
    landed = set()

    def land(slot):
        if slot not in landed:
            landed.add(slot)
            y_copy(slot).wait_recv()
            if slot >= SHARED:
                x_copy(slot).wait_recv()

    for number, group in enumerate(GROUPS):
        if number == FAR_AFTER:
            pl.semaphore_wait(ready.at[2], 1)
            send((13,))
        for slot in PASS_ON.get(number, ()):
            land(slot)
            y_copy(RELAY[slot], via=slot).start()
            if slot >= SHARED:
                x_copy(RELAY[slot], via=slot).start()
        if number == NEAR_AFTER:
            for slot in DIRECT:
                if slot < SHARED:
                    x_copy(slot).start()
        if number == NEAR_PASS_AFTER:
            for slot, there in RELAY.items():
                if slot < SHARED:
                    x_copy(slot).wait_recv()
                    x_copy(there, via=slot).start()
        for slot in group:
            land(slot)
        for slot in group:
            pltpu.make_async_copy(ybuf.at[slot], yh_ref.at[slot], keep.at[2]).start()
            if slot >= SHARED:
                pltpu.make_async_copy(xbuf.at[slot - SHARED], xh_ref.at[slot], keep.at[3]).start()
        work = []
        for slot in group:
            work.append((ybuf.at[slot], slot, xlhs, racc))
            if slot >= SHARED:
                work.append((xbuf.at[slot - SHARED], slot, ylhs, cacc))
        for spot, (shard, slot, lhs, acc) in enumerate(work):
            prepare(shard, spot)
        for spot, (shard, slot, lhs, acc) in enumerate(work):
            if slot < SHARED:
                shared_tile(spot, slot)
            else:
                row_tile(spot, lhs, acc)
        for slot in group:
            if slot < SHARED:
                c_copy(slot).start()

    def over_lanes(acc):
        parts = [jnp.sum(acc[128 * j : 128 * j + 128, :].T, axis=0, keepdims=True) for j in range(TILES)]
        return jnp.concatenate(parts, axis=0)

    rows = over_lanes(racc)
    columns = over_lanes(cacc) if SHARED < SLOTS else jnp.zeros((TILES, 128), jnp.float32)
    f, g, xl, yl = fin[...], gin[...], xlin[...], ylin[...]
    out_ref[0:6, :] = f + 0.5 * (xl - LN2 * jnp.log2(rows))
    all_of(cbuf, cr_sem, 1, SHARED - 1).wait()
    total = csend[0, :, :]
    for slot in range(1, SHARED):
        total = total + cbuf[slot, :, :]
    columns = columns + total[:TILES, :]
    out_ref[8:14, :] = g + 0.5 * (yl - LN2 * jnp.log2(columns))
    out_ref[16:22, :] = jnp.minimum(rows, columns)
    out_ref[24:30, :] = jnp.maximum(rows, columns)
    all_of(csend, cs_sem, 1, SHARED - 1).wait()
    all_of(ybuf, ysend, 1, SLOTS - 1).wait()
    all_of(xh_ref, xsend, 1, SHARED - 1).wait()
    for slot in range(1, SHARED):
        if slot not in RELAY:
            x_copy(slot).wait_recv()
    pltpu.make_async_copy(xs, xh_ref.at[0], keep.at[0]).wait()
    pltpu.make_async_copy(ys, yh_ref.at[0], keep.at[1]).wait()
    all_of(yh_ref, keep.at[2], 1, SLOTS - 1).wait()
    if SHARED < SLOTS:
        all_of(xbuf, farsend, 0, SLOTS - SHARED).wait()
        all_of(xh_ref, keep.at[3], SHARED, SLOTS - SHARED).wait()


def stable(own_pos_ref, others_hbm, shards, sem, lhs, rhs, top, acc, rows):
    copy = pltpu.make_async_copy(others_hbm, shards, sem)
    copy.start()
    for j in range(TILES):
        pos = own_pos_ref[:, 128 * j : 128 * j + 128]
        terms = own_terms(pos, jnp.zeros((1, 128), jnp.float32))
        rhs[:, 128 * j : 128 * j + 128] = terms.astype(jnp.bfloat16)
    top[...] = jnp.full_like(top, lowest)
    acc[...] = jnp.zeros_like(acc)
    copy.wait()

    def one(slot, carry):
        for j in range(TILES):
            terms = other_terms(shards[slot, 8 * j : 8 * j + 8, :], shards[slot, pl.ds(48 + j, 1), :])
            lhs[128 * j : 128 * j + 128, :] = terms.T.astype(jnp.bfloat16)
        for c in range(3):
            weights = rhs[:, 256 * c : 256 * c + 256]
            best, total = top[:, 256 * c : 256 * c + 256], acc[:, 256 * c : 256 * c + 256]
            for t in range(0, 768, 128):
                score = jnp.dot(lhs[t : t + 128, :], weights, preferred_element_type=jnp.float32)
                score = score.reshape(16, 8, 256)
                new = jnp.maximum(best, jnp.max(score, axis=0))
                total = total * jnp.exp2(best - new) + jnp.sum(jnp.exp2(score - new[None]), axis=0)
                best = new
            top[:, 256 * c : 256 * c + 256] = best
            acc[:, 256 * c : 256 * c + 256] = total
        return carry

    lax.fori_loop(0, SLOTS, one, 0)
    best = jnp.max(top[...], axis=0, keepdims=True)
    total = jnp.sum(acc[...] * jnp.exp2(top[...] - best), axis=0, keepdims=True)
    result = LN2 * (best + jnp.log2(total))
    for j in range(TILES):
        pos = own_pos_ref[:, 128 * j : 128 * j + 128]
        half = 0.5 * jnp.sum(pos * pos, axis=0, keepdims=True)
        rows[j : j + 1, :] = half - result[:, 128 * j : 128 * j + 128]


def finish_kernel(
    sums_ref, x_ref, y_ref, f_ref, g_ref, yh_ref, xh_ref,
    fo_ref, go_ref,
    own, pot, shards, lhs, rhs, top, acc, rows, sem,
):
    fo_ref[...] = sums_ref[0:6, :]
    go_ref[...] = sums_ref[8:14, :]
    least = jnp.min(sums_ref[16:22, :])
    most = jnp.max(sums_ref[24:30, :])

    @pl.when(jnp.logical_not(jnp.logical_and(least >= SMALL, most <= LARGE)))
    def _():
        for pos_hbm, pot_hbm, others_hbm, out in ((x_ref, f_ref, yh_ref, fo_ref), (y_ref, g_ref, xh_ref, go_ref)):
            for src, dst in ((pos_hbm, own), (pot_hbm, pot)):
                copy = pltpu.make_async_copy(src, dst, sem.at[0])
                copy.start()
                copy.wait()
            stable(own, others_hbm, shards, sem.at[1], lhs, rhs, top, acc, rows)
            out[...] = 0.5 * (pot[...] + rows[...])


def shards(x_pos, y_pos, f_pot, g_pot, x_logw, y_logw):
    f, g, xl, yl = (a.reshape(TILES, 128) for a in (f_pot, g_pot, x_logw, y_logw))
    small = jax.ShapeDtypeStruct((TILES, 128), jnp.float32)
    gathered = jax.ShapeDtypeStruct((SLOTS, ROWS, 128), jnp.float32)
    vmem = pl.BlockSpec(memory_space=pltpu.VMEM)
    anywhere = pl.BlockSpec(memory_space=pl.ANY)
    f32, bf16 = jnp.float32, jnp.bfloat16
    sums, yh, xh = pl.pallas_call(
        exchange_kernel,
        out_shape=(pltpu.VMEM((32, 128), f32), gathered, gathered),
        in_specs=[anywhere] * 6,
        out_specs=(vmem, anywhere, anywhere),
        scratch_shapes=[
            pltpu.VMEM((8, 768), f32),
            pltpu.VMEM((8, 768), f32),
            pltpu.VMEM((TILES, 128), f32),
            pltpu.VMEM((TILES, 128), f32),
            pltpu.VMEM((TILES, 128), f32),
            pltpu.VMEM((TILES, 128), f32),
            pltpu.VMEM((ROWS, 128), f32),
            pltpu.VMEM((ROWS, 128), f32),
            pltpu.VMEM((SLOTS, ROWS, 128), f32),
            pltpu.VMEM((max(SLOTS - SHARED, 1), ROWS, 128), f32),
            pltpu.VMEM((768, DEPTH), bf16),
            pltpu.VMEM((768, DEPTH), bf16),
            pltpu.VMEM((4, DEPTH, 768), bf16),
            pltpu.VMEM((768, 128), f32),
            pltpu.VMEM((768, 128), f32),
            pltpu.VMEM((SLOTS, 8, 128), f32),
            pltpu.VMEM((SLOTS, 8, 128), f32),
            pltpu.SemaphoreType.DMA((6,)),
            pltpu.SemaphoreType.DMA,
            pltpu.SemaphoreType.DMA((SLOTS,)),
            pltpu.SemaphoreType.DMA,
            pltpu.SemaphoreType.DMA((SLOTS,)),
            pltpu.SemaphoreType.DMA,
            pltpu.SemaphoreType.DMA,
            pltpu.SemaphoreType.DMA,
            pltpu.SemaphoreType.DMA((4,)),
            pltpu.SemaphoreType.REGULAR((3,)),
        ],
        compiler_params=pltpu.CompilerParams(collective_id=0, has_side_effects=True),
        name="exchange",
    )(x_pos, y_pos, f, g, xl, yl)
    fo, go = pl.pallas_call(
        finish_kernel,
        out_shape=(small, small),
        in_specs=[vmem] + [anywhere] * 6,
        out_specs=(vmem, vmem),
        scratch_shapes=[
            pltpu.VMEM((8, 768), f32),
            pltpu.VMEM((TILES, 128), f32),
            pltpu.VMEM((SLOTS, ROWS, 128), f32),
            pltpu.VMEM((768, DEPTH), bf16),
            pltpu.VMEM((DEPTH, 768), bf16),
            pltpu.VMEM((8, 768), f32),
            pltpu.VMEM((8, 768), f32),
            pltpu.VMEM((TILES, 128), f32),
            pltpu.SemaphoreType.DMA((2,)),
        ],
        name="finish",
    )(pltpu.with_memory_space_constraint(sums, pltpu.VMEM), x_pos, y_pos, f, g, yh, xh)
    return fo.reshape(-1), go.reshape(-1)


def solution(mesh):
    both = ("blk", "grp")
    return jax.shard_map(
        shards,
        mesh=mesh,
        in_specs=(P(None, both), P(None, both), P(both), P(both), P(both), P(both)),
        out_specs=(P(both), P(both)),
        check_vma=False,
    )
```

profile of v0, /device:TPU:0, one launch (start us, length us, event | category | flops | bytes accessed | tf_op | source)
XLA Modules:
  0.0 48.2 jit_solution(266452135295558933)
XLA Ops:
  0.6 20.6 %exchange.1 = (f32[32,128]{1,0:T(8,128)S(1)}, f32[16,56,128]{2,1,0:T(8,128)}, f32[16,56,128]{2,1,0:T(8,128)}) custom-call(f32[8,768]{1,0:T(8,128)} %x_ref.1, f32[8,768]{1,0:T(8,128)} %y_ref.1, f32[6,128]{1,0:T(8,128)} %bitcast.6, f32[6,128]{1,0:T(8,128)} %bitcast.8, f32[6,128]{1,0:T(8,128)} %bitcast.10, f32[6,128]{1,0:T(8,128)} %bitcast.11), custom_call_target="tpu_custom_call" | custom-call | tf_op jit(solution)/shard_map/exchange/pallas_call | solution.py:348
  21.3 26.9 %finish.1 = (f32[6,128]{1,0:T(8,128)}, f32[6,128]{1,0:T(8,128)}) custom-call(f32[32,128]{1,0:T(8,128)S(1)} %get-tuple-element.7.sums_ref, f32[8,768]{1,0:T(8,128)} %x_ref.1, f32[8,768]{1,0:T(8,128)} %y_ref.1, f32[6,128]{1,0:T(8,128)} %bitcast.7, f32[6,128]{1,0:T(8,128)} %bitcast.9, f32[16,56,128]{2,1,0:T(8,128)} %get-tuple-element.8.yh_ref, ...), custom_call_target="tpu_custom_call" | custom-call | tf_op jit(solution)/shard_map/finish/pallas_call | solution.py:385
where the time goes:
time: 48.6 us; the launch traced here: 48.2 us
  Pallas kernels  47.6 us (98%)
  between operations  0.64 us (1%)
    pallas_call x1, Pallas kernels, shards(): pl.pallas_call(finish_kernel, out_shape=(small, small), in_specs=[vmem] +...  26.9 us
    pallas_call x1, Pallas kernels, shards(): pl.pallas_call(exchange_kernel, out_shape=(pltpu.VMEM((32, 128), f32), ga...  20.6 us

commit v1 on v0

--- a/solution.py
+++ b/solution.py
@@ -23,7 +23,7 @@
 SHARED = 12
 GROUPS = ((1,), (2, 3), (6, 7), (8, 9), (4, 5), (10, 11), (12,), (13,), (14,), (15,))
 PASS_ON = {1: (2, 3), 2: (8,), 5: (12,), 6: (13,)}
-NEAR_AFTER, NEAR_PASS_AFTER, FAR_AFTER = (2, 5, 1)
+NEAR_AFTER, NEAR_PASS_AFTER, FAR_AFTER = (2, 6, 1)
 MESH = pl.DeviceIdType.MESH
 
 
@@ -111,10 +111,9 @@
     csend[...] = jnp.zeros_like(csend)
     racc[...] = jnp.zeros_like(racc)
     cacc[...] = jnp.zeros_like(cacc)
-    for copy in loads:
+    for copy in loads[:3]:
         copy.wait()
     pack_shard(yin, gin, ylin, ys)
-    pack_shard(xin, fin, xlin, xs)
     pl.semaphore_wait(barrier, len(greeted))
 
     def y_copy(slot, via=None):
@@ -163,6 +162,9 @@
             terms = own_terms(shard[8 * j : 8 * j + 8, :], shard[48 + j : 49 + j, :])
             lhs[128 * j : 128 * j + 128, :] = terms.T.astype(jnp.bfloat16)
 
+    for copy in loads[3:]:
+        copy.wait()
+    pack_shard(xin, fin, xlin, xs)
     own_side(xs, xlhs)
 
     def prepare(shard, spot):

time: 48.6 us -> 48.6 us (level)
  no operation moved by 1% of the time
where the time goes in v1:
time: 48.6 us; the launch traced here: 47.8 us
  Pallas kernels  47.2 us (97%)
  between operations  0.64 us (1%)
    pallas_call x1, Pallas kernels, shards(): pl.pallas_call(finish_kernel, out_shape=(small, small), in_specs=[vmem] +...  26.9 us
    pallas_call x1, Pallas kernels, shards(): pl.pallas_call(exchange_kernel, out_shape=(pltpu.VMEM((32, 128), f32), ga...  20.3 us

profile of v1, /device:TPU:0, one launch (start us, length us, event | category | flops | bytes accessed | tf_op | source)
XLA Modules:
  0.0 47.8 jit_solution(9914460971075786875)
XLA Ops:
  0.6 20.3 %exchange.1 = (f32[32,128]{1,0:T(8,128)S(1)}, f32[16,56,128]{2,1,0:T(8,128)}, f32[16,56,128]{2,1,0:T(8,128)}) custom-call(f32[8,768]{1,0:T(8,128)} %x_ref.1, f32[8,768]{1,0:T(8,128)} %y_ref.1, f32[6,128]{1,0:T(8,128)} %bitcast.6, f32[6,128]{1,0:T(8,128)} %bitcast.8, f32[6,128]{1,0:T(8,128)} %bitcast.10, f32[6,128]{1,0:T(8,128)} %bitcast.11), custom_call_target="tpu_custom_call" | custom-call | tf_op jit(solution)/shard_map/exchange/pallas_call | solution.py:350
  20.9 26.9 %finish.1 = (f32[6,128]{1,0:T(8,128)}, f32[6,128]{1,0:T(8,128)}) custom-call(f32[32,128]{1,0:T(8,128)S(1)} %get-tuple-element.7.sums_ref, f32[8,768]{1,0:T(8,128)} %x_ref.1, f32[8,768]{1,0:T(8,128)} %y_ref.1, f32[6,128]{1,0:T(8,128)} %bitcast.7, f32[6,128]{1,0:T(8,128)} %bitcast.9, f32[16,56,128]{2,1,0:T(8,128)} %get-tuple-element.8.yh_ref, ...), custom_call_target="tpu_custom_call" | custom-call | tf_op jit(solution)/shard_map/finish/pallas_call | solution.py:387
